TPU v7x, 32 devices: a whole 2x2x4 slice. The times are simulated.
32 devices in a mesh: lat: 4 (over x, core), lon: 8 (over z, y).
Axes of the slice: x: 2, y: 2, z: 4, core: 2. Of those that a mesh axis runs over, the one named last changes fastest.
Arguments:
- tokens: bfloat16 [1, 48, 96, 512], P(None, 'lat', 'lon'), may hold values from -8 to 8
- gain_first: float32 [512], replicated, may hold values from 0.1 to 1.9
- qkv_first: bfloat16 [512, 1536], replicated, may hold values from -16 to 16
- proj_first: bfloat16 [512, 512], replicated, may hold values from -0.25 to 0.25
- bias_first: float32 [4, 16, 529], P('lat'), may hold values from -6 to 6
- gain_second: float32 [512], replicated, may hold values from 0.1 to 1.9
- qkv_second: bfloat16 [512, 1536], replicated, may hold values from -16 to 16
- proj_second: bfloat16 [512, 512], replicated, may hold values from -0.25 to 0.25
- bias_second: float32 [4, 16, 529], P('lat'), may hold values from -6 to 6
Outputs:
- mixed: bfloat16 [1, 48, 96, 512], P(None, 'lat', 'lon')
All inputs are finite; a program needn't handle non-finite values.
Results may differ from a plain program's by a relative error of at most 0.012.
The roundings to bfloat16 on the way count: a program that leaves them out, or rounds other values in their place, can miss the bound.
Values may be sent and summed in bfloat16 or wider, within the bound.
No kernel may reach another device: no remote copies, remote signals or barrier semaphores. Data moves between devices by JAX's collectives and lax.ppermute only.
A program may use at most 64 MiB of HBM per device.

v0:
```python
import functools
import math

import jax
import jax.numpy as jnp
from jax import lax
from jax.experimental import pallas as pl
from jax.experimental.pallas import tpu as pltpu
from jax.sharding import PartitionSpec as P


HEADS = 16
CUTS = 4
CUT_FROM = 1 << 19
WH = 12
WW = 12
LANES = 128
SUB = 8
PITCH = 16
SPAN_C = 2 * WW - 1
HALF_R = WH // 2
HALF_C = WW // 2
REST = WW - SUB
NEG = -1e30
LOG2E = math.log2(math.e)
F32 = jnp.float32
BF16 = jnp.bfloat16


def iota(shape, dim):
    return lax.broadcasted_iota(jnp.int32, shape, dim)


def bias_strips(table, tab, strips):
    heads = table.shape[1]
    count = table.shape[2]
    tab[...] = jnp.zeros_like(tab)
    tab[:, :count] = table[0]
    lane = iota((SUB, LANES), 1)
    row = iota((SUB, LANES), 0)
    plans = []
    for tile in range(2):
        for k in range(3):
            u = lane + k * LANES
            step = u // PITCH
            if tile == 0:
                col = row
            else:
                second = row >= REST
                col = SUB + jnp.where(second, row - REST, row)
                step = jnp.where(second, step - 1, step)
            index = step * SPAN_C + u % PITCH - col + WW - 1
            index = jnp.clip(index, 0, count - 1)
            low = max(8 * k - tile, 0) * SPAN_C
            top = min((8 * k + 7) * SPAN_C + PITCH + WW - 2, count - 1)
            sources = range(low // LANES, top // LANES + 1)
            plans.append((tile, k, index % LANES, index // LANES, sources))
    for tile, k, inner, outer, sources in plans:
        values = [None] * heads
        for s in sources:
            here = outer == s
            for h in range(heads):
                row = jnp.broadcast_to(tab[h : h + 1, s * LANES : (s + 1) * LANES], (SUB, LANES))
                taken = jnp.take_along_axis(row, inner, axis=1)
                values[h] = taken if values[h] is None else jnp.where(here, taken, values[h])
        for h in range(heads):
            strips[h, tile, :, k * LANES : (k + 1) * LANES] = values[h] * LOG2E


def bias_tiles(strips, h):
    turned = {}
    lane = iota((SUB, LANES), 1)
    per_head = WH * PITCH

    def turn(head, tile, k, by):
        key = (head, tile, k, by)
        if key not in turned:
            part = strips[head, tile, :, k * LANES : (k + 1) * LANES]
            turned[key] = pltpu.roll(part, LANES - by, 1) if by else part
        return turned[key]

    def window(tile, start, t):
        cuts = []
        at = t * LANES
        while at < (t + 1) * LANES:
            which, query = divmod(at, per_head)
            u = start + query
            k = u // LANES
            end = min(at + (k + 1) * LANES - u, (which + 1) * per_head, (t + 1) * LANES)
            cuts.append((end - t * LANES, turn(h + which, tile, k, (u - at) % LANES)))
            at = end
        value = cuts[-1][1]
        for end, part in reversed(cuts[:-1]):
            value = jnp.where(lane < end, part, value)
        return value

    starts = [(0, PITCH * (WH - 1 - r)) for r in range(WH)]
    starts += [(1, PITCH * (WH - 1 - r)) for r in range(0, WH, 2)]
    return [[window(tile, start, t) for tile, start in starts] for t in range(2 * per_head // LANES)]


def halves(polar):
    lane = iota((SUB, LANES), 1)
    out = []
    for t in range(2 * WH * PITCH // LANES):
        query = (lane + t * LANES) % (WH * PITCH) // PITCH >= HALF_R
        out.append([jnp.where((query != lower) & polar, NEG, 0.0).astype(F32) for lower in (False, True)])
    return out


def compact(value):
    width = value.shape[-1]
    tiles = value.reshape(WH, 2, SUB, width)
    row = iota((SUB, width), 0)
    parts = [tiles[r, 0] for r in range(WH)]
    for r in range(0, WH, 2):
        parts.append(jnp.where(row < REST, tiles[r, 1], pltpu.roll(tiles[r + 1, 1], REST, 0)))
    return jnp.concatenate(parts, axis=0)


def spread(value):
    width = value.shape[-1]
    tiles = value.reshape(WH * WW // SUB, SUB, width)
    parts = []
    for r in range(WH):
        rest = tiles[WH + r // 2]
        parts += [tiles[r], pltpu.roll(rest, REST, 0) if r % 2 else rest]
    return jnp.concatenate(parts, axis=0)


def split(value):
    high = value.astype(BF16)
    return high, (value - high.astype(F32)).astype(BF16)


def soft(scores, bias, probs, at):
    count = len(bias)
    tiles = [scores[u * SUB : (u + 1) * SUB] + bias[u] for u in range(count)]
    top = functools.reduce(jnp.maximum, tiles)
    top = jnp.max(top, axis=0, keepdims=True)
    tiles = [jnp.exp2(s - top) for s in tiles]
    total = functools.reduce(jnp.add, tiles)
    inverse = 1.0 / jnp.sum(total, axis=0, keepdims=True)
    for u in range(0, count, 2):
        pair = jnp.concatenate([tiles[u] * inverse, tiles[u + 1] * inverse], axis=0)
        probs[u * SUB : (u + 2) * SUB, at : at + LANES] = pair.astype(BF16)


def attend(xs, ys, gain, weights, tiles_of, probs):
    width = xs.shape[-1]
    head_dim = width // HEADS
    group = LANES // head_dim
    per_head = WH * PITCH
    x = compact(xs[...].reshape(per_head, width))
    mean = jnp.mean(x, axis=-1, keepdims=True)
    centred = x - mean
    var = jnp.mean(centred * centred, axis=-1, keepdims=True)
    normed = centred * lax.rsqrt(var + 1e-05) * gain[...]
    spread_out = spread(normed).astype(BF16)
    normed = normed.astype(BF16)
    wqkv = weights(0)
    query = jnp.dot(spread_out, wqkv[:, :width], preferred_element_type=F32)
    mixed = jnp.dot(normed, wqkv[:, width:], preferred_element_type=F32)
    q_hi, q_lo = split(query * (head_dim ** (-0.5) * LOG2E))
    k_hi, k_lo = split(mixed[:, :width])
    values = mixed[:, width:].astype(BF16)
    lane = iota((1, LANES), 1)

    def product(g):
        part = slice(g * LANES, (g + 1) * LANES)
        left = jnp.concatenate([k_hi[:, part], k_hi[:, part], k_lo[:, part]], axis=1)
        rights = []
        for i in range(group):
            own = (lane // head_dim == i).astype(BF16)
            high = q_hi[:, part] * own
            rights.append(jnp.concatenate([high, q_lo[:, part] * own, high], axis=1))
        right = jnp.concatenate(rights, axis=0)
        return lax.dot_general(left, right, (((1,), (1,)), ((), ())), preferred_element_type=F32)

    def gather(g):
        part = slice(g * LANES, (g + 1) * LANES)
        turned = values[:, part].T
        heads_out = []
        for i in range(0, group, 2):
            mixed_v = jnp.dot(
                turned[i * head_dim : (i + 2) * head_dim],
                probs[g, :, i * per_head : (i + 2) * per_head],
                preferred_element_type=F32,
            )
            heads_out.append(mixed_v[:head_dim, : 2 * LANES])
            heads_out.append(pltpu.roll(mixed_v[head_dim:, LANES:], 2 * LANES - per_head % LANES, 1))
        return jnp.concatenate(heads_out, axis=0).astype(BF16).T

    outs = []
    groups = HEADS // group
    ahead = product(0)
    for g in range(groups):
        scores = ahead
        if g + 1 < groups:
            ahead = product(g + 1)
        if g:
            outs.append(gather(g - 1))
        for i in range(0, group, 2):
            tiles = tiles_of(g * group + i)
            for t in range(len(tiles)):
                at = i * per_head + t * LANES
                soft(scores[:, at : at + LANES], tiles[t], probs.at[g], at)
    outs.append(gather(groups - 1))
    heads_out = jnp.concatenate(outs, axis=1)[:per_head]
    wproj = weights(1)
    branch = jnp.dot(heads_out, wproj[...], preferred_element_type=F32)
    ys[...] = xs[...] + branch.reshape(xs.shape)


CORNERS = [(r, c) for r in (0, HALF_R) for c in (0, HALF_C)]


def quadrants(ys, outs):
    for at, (r, c) in enumerate(CORNERS):
        outs[at][...] = ys[r : r + HALF_R, c : c + HALF_C, :].astype(BF16)


def packed(ys, zs, outs):
    for at, (r, c) in enumerate(CORNERS):
        for i in range(HALF_R):
            zs[at, i * HALF_C : (i + 1) * HALF_C, :] = ys[r + i, c : c + HALF_C, :]
        outs[at][...] = zs[at].astype(BF16)


def unpacked(pieces, zs, xs):
    for at, (r, c) in enumerate(CORNERS):
        zs[at] = pieces[at][...].astype(F32)
        for i in range(HALF_R):
            xs[r + i, c : c + HALF_C, :] = zs[at, i * HALF_C : (i + 1) * HALF_C, :]


def cuts(shape):
    if len(shape) == 2 and shape[0] * shape[1] >= CUT_FROM:
        rows = shape[0] // CUTS
        return [pl.ds(i * rows, rows) for i in range(CUTS)]
    return [slice(None)]


def pieces_of(source, target):
    return [(source.at[part], target.at[part]) for part in cuts(source.shape)]


def first_kernel(tokens, table, gain, wqkv, wproj, nw, ne, sw, se, xs, ys, zs, probs, tab, strips, *here):
    here, sems = here[:-1], here[-1]
    pairs = [pair for a, b in zip((table, tokens, gain, wqkv, wproj), here) for pair in pieces_of(a, b)]
    copies = [pltpu.make_async_copy(a, b, sems.at[i]) for i, (a, b) in enumerate(pairs)]
    for copy in copies:
        copy.start()
    xs[:, WW:, :] = jnp.zeros((WH, PITCH - WW, xs.shape[-1]), F32)
    copies[0].wait()
    bias_strips(here[0], tab, strips)
    copies[1].wait()
    xs[:, :WW, :] = here[1][0].astype(F32)
    copies[2].wait()

    def weights(i):
        for copy in (copies[3:-1], copies[-1:])[i]:
            copy.wait()
        return here[3 + i]

    attend(xs, ys, here[2], weights, functools.partial(bias_tiles, strips), probs)
    packed(ys, zs, (nw, ne, sw, se))


def bias_kernel(table, out, tab, strips):
    masks = halves(lax.axis_index("lat") == lax.axis_size("lat") - 1)
    bias_strips(table, tab, strips)
    for pair in range(out.shape[0]):
        for t, tiles in enumerate(bias_tiles(strips, 2 * pair)):
            for u, tile in enumerate(tiles):
                lower = u >= HALF_R if u < WH else 2 * (u - WH) >= HALF_R
                out[pair, t, u] = tile + masks[t][int(lower)]


def second_kernel(nw_in, ne_in, sw_in, se_in, bias, gain, wqkv, wproj, nw, ne, sw, se, xs, ys, zs, probs):
    xs[:, WW:, :] = jnp.zeros((WH, PITCH - WW, xs.shape[-1]), F32)
    unpacked((nw_in, ne_in, sw_in, se_in), zs, xs)

    def tiles_of(h):
        return [[bias[h // 2, t, u] for u in range(bias.shape[2])] for t in range(bias.shape[1])]

    attend(xs, ys, gain, lambda i: (wqkv, wproj)[i], tiles_of, probs)
    quadrants(ys, (nw, ne, sw, se))


VMEM = pl.BlockSpec(memory_space=pltpu.VMEM)
HBM = pl.BlockSpec(memory_space=pltpu.HBM)


def bias_room(table):
    _, heads, count = table.shape
    lanes = -(-count // LANES) * LANES
    return [pltpu.VMEM((heads, lanes), F32), pltpu.VMEM((heads, 2, SUB, 3 * LANES), F32)]


def expand(table):
    heads = table.shape[1]
    lane_tiles = 2 * WH * PITCH // LANES
    shape = (heads // 2, lane_tiles, WH * WW // SUB, SUB, LANES)
    return pl.pallas_call(
        bias_kernel,
        out_shape=jax.ShapeDtypeStruct(shape, F32),
        in_specs=[VMEM],
        out_specs=VMEM,
        scratch_shapes=bias_room(table),
        compiler_params=pltpu.CompilerParams(vmem_limit_bytes=8 << 20),
        cost_estimate=pl.CostEstimate(flops=2_000_000, bytes_accessed=1_800_000, transcendentals=0),
    )(table)


def block(kernel, pieces, bias, gain, wqkv, wproj, fetch, shape):
    width = wproj.shape[0]
    group = LANES * HEADS // width
    piece = jax.ShapeDtypeStruct(shape, BF16)
    args = (*pieces, bias, gain.reshape(1, width), wqkv, wproj)
    scratch = [
        pltpu.VMEM((WH, PITCH, width), F32),
        pltpu.VMEM((WH, PITCH, width), F32),
        pltpu.VMEM((4, HALF_R * HALF_C, width), F32),
        pltpu.VMEM((HEADS // group, WH * WW, group * WH * PITCH), BF16),
    ]
    if fetch:
        order = (args[1], args[0], *args[2:])
        scratch += bias_room(bias)
        scratch += [pltpu.VMEM(a.shape, a.dtype) for a in order]
        scratch += [pltpu.SemaphoreType.DMA((sum(len(cuts(a.shape)) for a in order),))]
        args = tuple(pltpu.with_memory_space_constraint(a, pltpu.HBM) for a in args)
    source = HBM if fetch else VMEM
    return pl.pallas_call(
        kernel,
        out_shape=(pltpu.VMEM(shape, BF16) if fetch else piece,) * 4,
        in_specs=[source] * len(args),
        out_specs=(VMEM,) * 4,
        scratch_shapes=scratch,
        compiler_params=pltpu.CompilerParams(vmem_limit_bytes=(63 if fetch else 24) << 20),
        cost_estimate=pl.CostEstimate(flops=400_000_000, bytes_accessed=2_500_000, transcendentals=600_000),
    )(*args)


def moved(piece, lat, lon):
    rows, cols = lax.axis_size("lat"), lax.axis_size("lon")
    route = [
        (((i + lat) % rows) * cols + (j + lon) % cols, i * cols + j) for i in range(rows) for j in range(cols)
    ]
    return lax.ppermute(piece, ("lat", "lon"), route)


def shards(
    tokens,
    gain_first,
    qkv_first,
    proj_first,
    bias_first,
    gain_second,
    qkv_second,
    proj_second,
    bias_second,
):
    size = (HALF_R * HALF_C, tokens.shape[-1])
    nw, ne, sw, se = block(
        first_kernel, (tokens,), bias_first, gain_first, qkv_first, proj_first, True, size
    )
    bias = expand(bias_second)
    window = (se, moved(sw, 0, 1), moved(ne, 1, 0), moved(nw, 1, 1))
    size = (HALF_R, HALF_C, tokens.shape[-1])
    nw, ne, sw, se = block(second_kernel, window, bias, gain_second, qkv_second, proj_second, False, size)
    west, north, corner = moved(ne, 0, -1), moved(sw, -1, 0), moved(se, -1, -1)
    upper = jnp.concatenate([corner, north], axis=1)
    lower = jnp.concatenate([west, nw], axis=1)
    return jnp.concatenate([upper, lower], axis=0)[None]


def solution(mesh):
    placed = (
        P(None, "lat", "lon", None),
        P(),
        P(),
        P(),
        P("lat", None, None),
        P(),
        P(),
        P(),
        P("lat", None, None),
    )
    return jax.shard_map(
        shards, mesh=mesh, in_specs=placed, out_specs=P(None, "lat", "lon", None), check_vma=False
    )
```

profile of v0, /device:TPU:0, one launch (start us, length us, event | category | flops | bytes accessed | tf_op | source)
XLA Modules:
  0.0 25.1 jit_solution(12580722662756266132)
XLA Ops:
  0.0 0.0 copy-start.2
  0.0 0.0 copy-start.1
  0.0 0.0 copy-start.3
  0.0 3.7 %shard_map.91 = (bf16[36,512]{1,0:T(8,128)(2,1)S(1)}, bf16[36,512]{1,0:T(8,128)(2,1)S(1)}, bf16[36,512]{1,0:T(8,128)(2,1)S(1)}, bf16[36,512]{1,0:T(8,128)(2,1)S(1)}) custom-call(bf16[1,12,12,512]{3,2,1,0:T(8,128)(2,1)} %tokens.1, f32[1,16,529]{2,1,0:T(8,128)} %table.2, f32[1,512]{1,0:T(1,128)} %bitcast.5, bf16[512,1536]{1,0:T(8,128)(2,1)} %wqkv.2, ...), custom_call_target="tpu_custom_call" | custom-call | flops 400000000 | bytes 2500000 | tf_op jit(solution)/shard_map/pallas_call | solution.py:334
  3.7 0.0 copy-start
  3.7 6.1 %collective-permute-start = (bf16[36,512]{1,0:T(8,128)(2,1)S(1)}, bf16[36,512]{1,0:T(8,128)(2,1)S(1)}, u32[]{:S(2)}, u32[]{:S(2)}) collective-permute-start(bf16[36,512]{1,0:T(8,128)(2,1)S(1)} %get-tuple-element.14), channel_id=1, source_target_pairs={{1,0},{2,1},{3,2},{4,3},{5,4},{6,5},{7,6},{0,7},{9,8},{10,9},{11,1... | collective-permute-start | bytes 110600 | tf_op jit(solution)/shard_map/ppermute | solution.py:350
  9.8 0.6 %collective-permute-start.1 = (bf16[36,512]{1,0:T(8,128)(2,1)S(1)}, bf16[36,512]{1,0:T(8,128)(2,1)S(1)}, u32[]{:S(2)}, u32[]{:S(2)}) collective-permute-start(bf16[36,512]{1,0:T(8,128)(2,1)S(1)} %get-tuple-element.15), channel_id=1, source_target_pairs={{8,0},{9,1},{10,2},{11,3},{12,4},{13,5},{14,6},{15,7},{16,8},{17,9... | collective-permute-start | bytes 110600 | tf_op jit(solution)/shard_map/ppermute | solution.py:350
  10.4 0.9 %collective-permute-start.2 = (bf16[36,512]{1,0:T(8,128)(2,1)S(1)}, bf16[36,512]{1,0:T(8,128)(2,1)S(1)}, u32[]{:S(2)}, u32[]{:S(2)}) collective-permute-start(bf16[36,512]{1,0:T(8,128)(2,1)S(1)} %get-tuple-element.16), channel_id=1, source_target_pairs={{9,0},{10,1},{11,2},{12,3},{13,4},{14,5},{15,6},{8,7},{17,8},{18,9... | collective-permute-start | bytes 110600 | tf_op jit(solution)/shard_map/ppermute | solution.py:350
  11.3 0.0 copy-done.2
  11.3 0.9 %shard_map.92.bias = f32[8,3,18,8,128]{4,3,2,1,0:T(8,128)S(1)} custom-call(f32[1,16,529]{2,1,0:T(8,128)S(1)} %copy-done.2), custom_call_target="tpu_custom_call" | custom-call | flops 2000000 | bytes 1800000 | tf_op jit(solution)/shard_map/pallas_call | solution.py:305
  12.3 0.0 collective-permute-done.ne_in
  12.3 0.0 collective-permute-done.1.sw_in
  12.3 1.6 %collective-permute-done.2.se_in = bf16[36,512]{1,0:T(8,128)(2,1)S(1)} collective-permute-done((bf16[36,512]{1,0:T(8,128)(2,1)S(1)}, bf16[36,512]{1,0:T(8,128)(2,1)S(1)}, u32[]{:S(2)}, u32[]{:S(2)}) %collective-permute-start.2) | collective-permute-done | bytes 36896 | tf_op jit(solution)/shard_map/ppermute | solution.py:350
  13.9 0.0 copy-done.1
  13.9 0.0 copy-done.3
  13.9 0.0 copy-done
  13.9 2.1 %shard_map.93 = (bf16[6,6,512]{2,1,0:T(8,128)(2,1)S(1)}, bf16[6,6,512]{2,1,0:T(8,128)(2,1)S(1)}, bf16[6,6,512]{2,1,0:T(8,128)(2,1)S(1)}, bf16[6,6,512]{2,1,0:T(8,128)(2,1)S(1)}) custom-call(bf16[36,512]{1,0:T(8,128)(2,1)S(1)} %get-tuple-element.13.nw_in, bf16[36,512]{1,0:T(8,128)(2,1)S(1)} %collective-permute-done.ne_in, ...), custom_call_target="tpu_custom_call" | custom-call | flops 400000000 | bytes 2500000 | tf_op jit(solution)/shard_map/pallas_call | solution.py:334
  16.0 0.1 collective-permute-start.3
  16.1 0.8 %collective-permute-start.4 = (bf16[6,6,512]{2,1,0:T(8,128)(2,1)S(1)}, bf16[6,6,512]{2,1,0:T(8,128)(2,1)S(1)}, u32[]{:S(2)}, u32[]{:S(2)}) collective-permute-start(bf16[6,6,512]{2,1,0:T(8,128)(2,1)S(1)} %get-tuple-element.18), channel_id=1, source_target_pairs={{24,0},{25,1},{26,2},{27,3},{28,4},{29,5},{30,6},{31,7},{0,8},{1,9... | collective-permute-start | bytes 110600 | tf_op jit(solution)/shard_map/ppermute | solution.py:350
  16.9 0.0 collective-permute-start.5
  16.9 6.7 %collective-permute-done.3 = bf16[6,6,512]{2,1,0:T(8,128)(2,1)S(1)} collective-permute-done((bf16[6,6,512]{2,1,0:T(8,128)(2,1)S(1)}, bf16[6,6,512]{2,1,0:T(8,128)(2,1)S(1)}, u32[]{:S(2)}, u32[]{:S(2)}) %collective-permute-start.3) | collective-permute-done | bytes 36896 | tf_op jit(solution)/shard_map/ppermute | solution.py:350
  23.6 0.0 collective-permute-done.4
  23.6 0.7 %collective-permute-done.5 = bf16[6,6,512]{2,1,0:T(8,128)(2,1)S(1)} collective-permute-done((bf16[6,6,512]{2,1,0:T(8,128)(2,1)S(1)}, bf16[6,6,512]{2,1,0:T(8,128)(2,1)S(1)}, u32[]{:S(2)}, u32[]{:S(2)}) %collective-permute-start.5) | collective-permute-done | bytes 36896 | tf_op jit(solution)/shard_map/ppermute | solution.py:350
  24.3 0.7 %maximum_bitcast_fusion = bf16[1,12,12,512]{3,2,1,0:T(8,128)(2,1)} fusion(bf16[6,6,512]{2,1,0:T(8,128)(2,1)S(1)} %get-tuple-element.20, bf16[6,6,512]{2,1,0:T(8,128)(2,1)S(1)} %collective-permute-done.5, bf16[6,6,512]{2,1,0:T(8,128)(2,1)S(1)} %collective-permute-done.4, bf16[6,6,512]{2,1,0:T(8,128)(2,1)S(1)} %collective-permute-done.3), kind=kLoop, calls=%fused_computation | loop fusion | flops 589824 | bytes 294912 | tf_op jit(solution)/shard_map/broadcast_in_dim | solution.py:375
Async XLA Ops:
  0.0 11.3 %copy-start.2 = (f32[1,16,529]{2,1,0:T(8,128)S(1)}, f32[1,16,529]{2,1,0:T(8,128)}, u32[]{:S(2)}) copy-start(f32[1,16,529]{2,1,0:T(8,128)} %table.3) | copy-start | bytes 101572
  0.0 13.9 %copy-start.1 = (bf16[512,512]{1,0:T(8,128)(2,1)S(1)}, bf16[512,512]{1,0:T(8,128)(2,1)}, u32[]{:S(2)}) copy-start(bf16[512,512]{1,0:T(8,128)(2,1)} %wproj.3) | copy-start | bytes 1572868
  0.0 13.9 %copy-start.3 = (f32[512]{0:T(512)S(1)}, f32[512]{0:T(512)}, u32[]{:S(2)}) copy-start(f32[512]{0:T(512)} %param.14) | copy-start | bytes 6148
  3.7 10.2 %copy-start = (bf16[512,1536]{1,0:T(8,128)(2,1)S(1)}, bf16[512,1536]{1,0:T(8,128)(2,1)}, u32[]{:S(2)}) copy-start(bf16[512,1536]{1,0:T(8,128)(2,1)} %wqkv.3) | copy-start | bytes 4718596
  3.7 8.6 %collective-permute-start = (bf16[36,512]{1,0:T(8,128)(2,1)S(1)}, bf16[36,512]{1,0:T(8,128)(2,1)S(1)}, u32[]{:S(2)}, u32[]{:S(2)}) collective-permute-start(bf16[36,512]{1,0:T(8,128)(2,1)S(1)} %get-tuple-element.14), channel_id=1, source_target_pairs={{1,0},{2,1},{3,2},{4,3},{5,4},{6,5},{7,6},{0,7},{9,8},{10,9},{11,1... | collective-permute-start | bytes 110600 | tf_op jit(solution)/shard_map/ppermute | solution.py:350
  9.8 2.5 %collective-permute-start.1 = (bf16[36,512]{1,0:T(8,128)(2,1)S(1)}, bf16[36,512]{1,0:T(8,128)(2,1)S(1)}, u32[]{:S(2)}, u32[]{:S(2)}) collective-permute-start(bf16[36,512]{1,0:T(8,128)(2,1)S(1)} %get-tuple-element.15), channel_id=1, source_target_pairs={{8,0},{9,1},{10,2},{11,3},{12,4},{13,5},{14,6},{15,7},{16,8},{17,9... | collective-permute-start | bytes 110600 | tf_op jit(solution)/shard_map/ppermute | solution.py:350
  10.4 3.4 %collective-permute-start.2 = (bf16[36,512]{1,0:T(8,128)(2,1)S(1)}, bf16[36,512]{1,0:T(8,128)(2,1)S(1)}, u32[]{:S(2)}, u32[]{:S(2)}) collective-permute-start(bf16[36,512]{1,0:T(8,128)(2,1)S(1)} %get-tuple-element.16), channel_id=1, source_target_pairs={{9,0},{10,1},{11,2},{12,3},{13,4},{14,5},{15,6},{8,7},{17,8},{18,9... | collective-permute-start | bytes 110600 | tf_op jit(solution)/shard_map/ppermute | solution.py:350
  16.0 7.6 %collective-permute-start.3 = (bf16[6,6,512]{2,1,0:T(8,128)(2,1)S(1)}, bf16[6,6,512]{2,1,0:T(8,128)(2,1)S(1)}, u32[]{:S(2)}, u32[]{:S(2)}) collective-permute-start(bf16[6,6,512]{2,1,0:T(8,128)(2,1)S(1)} %get-tuple-element.17), channel_id=1, source_target_pairs={{31,0},{24,1},{25,2},{26,3},{27,4},{28,5},{29,6},{30,7},{7,8},{0,9... | collective-permute-start | bytes 110600 | tf_op jit(solution)/shard_map/ppermute | solution.py:350
  16.1 7.6 %collective-permute-start.4 = (bf16[6,6,512]{2,1,0:T(8,128)(2,1)S(1)}, bf16[6,6,512]{2,1,0:T(8,128)(2,1)S(1)}, u32[]{:S(2)}, u32[]{:S(2)}) collective-permute-start(bf16[6,6,512]{2,1,0:T(8,128)(2,1)S(1)} %get-tuple-element.18), channel_id=1, source_target_pairs={{24,0},{25,1},{26,2},{27,3},{28,4},{29,5},{30,6},{31,7},{0,8},{1,9... | collective-permute-start | bytes 110600 | tf_op jit(solution)/shard_map/ppermute | solution.py:350
  16.9 7.5 %collective-permute-start.5 = (bf16[6,6,512]{2,1,0:T(8,128)(2,1)S(1)}, bf16[6,6,512]{2,1,0:T(8,128)(2,1)S(1)}, u32[]{:S(2)}, u32[]{:S(2)}) collective-permute-start(bf16[6,6,512]{2,1,0:T(8,128)(2,1)S(1)} %get-tuple-element.19), channel_id=1, source_target_pairs={{7,0},{0,1},{1,2},{2,3},{3,4},{4,5},{5,6},{6,7},{15,8},{8,9},{9,10... | collective-permute-start | bytes 110600 | tf_op jit(solution)/shard_map/ppermute | solution.py:350
where the time goes:
time: 25.2 us; the launch traced here: 25.1 us
  waiting for transfers between devices  9.05 us (36%)
  starting transfers between devices  8.52 us (34%)
  Pallas kernels  6.7 us (27%)
  other arithmetic  0.74 us (3%)
    ppermute x6, waiting for transfers between devices, moved(): return lax.ppermute(piece, ('lat', 'lon'), route)  9.05 us
    ppermute x6, starting transfers between devices, moved(): return lax.ppermute(piece, ('lat', 'lon'), route)  8.52 us
    pallas_call x2, Pallas kernels, block(): pl.pallas_call(kernel, out_shape=(pltpu.VMEM(shape, BF16) if fetch else p...  5.78 us
    pallas_call x1, Pallas kernels, expand(): pl.pallas_call(bias_kernel, out_shape=jax.ShapeDtypeStruct(shape, F32), i...  0.92 us
    broadcast_in_dim x1, other arithmetic, shards(): return jnp.concatenate([upper, lower], axis=0)[None]  0.74 us
  transfers between devices with their start and end apart: 6, of which 3 were waited for; matrix products, arithmetic and copies ran while one was open for 0% of the time, Pallas kernels for 4%

commit v1 on v0

--- a/solution.py
+++ b/solution.py
@@ -10,7 +10,7 @@
 
 
 HEADS = 16
-CUTS = 4
+CUTS = 2
 CUT_FROM = 1 << 19
 WH = 12
 WW = 12
@@ -215,11 +215,6 @@
 CORNERS = [(r, c) for r in (0, HALF_R) for c in (0, HALF_C)]
 
 
-def quadrants(ys, outs):
-    for at, (r, c) in enumerate(CORNERS):
-        outs[at][...] = ys[r : r + HALF_R, c : c + HALF_C, :].astype(BF16)
-
-
 def packed(ys, zs, outs):
     for at, (r, c) in enumerate(CORNERS):
         for i in range(HALF_R):
@@ -285,7 +280,7 @@
         return [[bias[h // 2, t, u] for u in range(bias.shape[2])] for t in range(bias.shape[1])]
 
     attend(xs, ys, gain, lambda i: (wqkv, wproj)[i], tiles_of, probs)
-    quadrants(ys, (nw, ne, sw, se))
+    packed(ys, zs, (nw, ne, sw, se))
 
 
 VMEM = pl.BlockSpec(memory_space=pltpu.VMEM)
@@ -342,6 +337,26 @@
     )(*args)
 
 
+def join_kernel(nw, ne, sw, se, out, ys, zs):
+    unpacked((nw, ne, sw, se), zs, ys)
+    out[0] = ys[:, :WW, :].astype(BF16)
+
+
+def join(*pieces):
+    width = pieces[0].shape[-1]
+    return pl.pallas_call(
+        join_kernel,
+        out_shape=jax.ShapeDtypeStruct((1, WH, WW, width), BF16),
+        in_specs=[VMEM] * 4,
+        out_specs=VMEM,
+        scratch_shapes=[
+            pltpu.VMEM((WH, PITCH, width), F32),
+            pltpu.VMEM((4, HALF_R * HALF_C, width), F32),
+        ],
+        compiler_params=pltpu.CompilerParams(vmem_limit_bytes=8 << 20),
+    )(*pieces)
+
+
 def moved(piece, lat, lon):
     rows, cols = lax.axis_size("lat"), lax.axis_size("lon")
     route = [
@@ -367,12 +382,9 @@
     )
     bias = expand(bias_second)
     window = (se, moved(sw, 0, 1), moved(ne, 1, 0), moved(nw, 1, 1))
-    size = (HALF_R, HALF_C, tokens.shape[-1])
     nw, ne, sw, se = block(second_kernel, window, bias, gain_second, qkv_second, proj_second, False, size)
     west, north, corner = moved(ne, 0, -1), moved(sw, -1, 0), moved(se, -1, -1)
-    upper = jnp.concatenate([corner, north], axis=1)
-    lower = jnp.concatenate([west, nw], axis=1)
-    return jnp.concatenate([upper, lower], axis=0)[None]
+    return join(corner, north, west, nw)
 
 
 def solution(mesh):

time: 25.2 us -> 24.9 us (0.988)
  Pallas kernels: 6.7 us -> 7.5 us
  other arithmetic: 0.74 us -> 0 us
  waiting for transfers between devices: 9.05 us -> 8.65 us
    pallas_call x0 -> x1, Pallas kernels: none -> 0.77 us  [join(): pl.pallas_call(join_kernel, out_shape=jax.ShapeDtypeStruct((1, WH, WW, wi...]
    broadcast_in_dim x1 -> x0, other arithmetic: 0.74 us -> none  [shards(): return jnp.concatenate([upper, lower], axis=0)[None]]
    ppermute x6, waiting for transfers between devices: 9.05 us -> 8.65 us  [moved(): return lax.ppermute(piece, ('lat', 'lon'), route)]
where the time goes in v1:
time: 24.9 us; the launch traced here: 24.7 us
  waiting for transfers between devices  8.65 us (35%)
  starting transfers between devices  8.52 us (34%)
  Pallas kernels  7.5 us (30%)
    ppermute x6, waiting for transfers between devices, moved(): return lax.ppermute(piece, ('lat', 'lon'), route)  8.65 us
    ppermute x6, starting transfers between devices, moved(): return lax.ppermute(piece, ('lat', 'lon'), route)  8.52 us
    pallas_call x2, Pallas kernels, block(): pl.pallas_call(kernel, out_shape=(pltpu.VMEM(shape, BF16) if fetch else p...  5.81 us
    pallas_call x1, Pallas kernels, expand(): pl.pallas_call(bias_kernel, out_shape=jax.ShapeDtypeStruct(shape, F32), i...  0.92 us
    pallas_call x1, Pallas kernels, join(): pl.pallas_call(join_kernel, out_shape=jax.ShapeDtypeStruct((1, WH, WW, wi...  0.77 us
  transfers between devices with their start and end apart: 6, of which 3 were waited for; matrix products, arithmetic and copies ran while one was open for 0% of the time, Pallas kernels for 4%

profile of v1, /device:TPU:0, one launch (start us, length us, event | category | flops | bytes accessed | tf_op | source)
XLA Modules:
  0.0 24.7 jit_solution(17047675361799848474)
XLA Ops:
  0.0 0.0 copy-start.2
  0.0 0.0 copy-start.1
  0.0 0.0 copy-start.3
  0.0 3.7 %shard_map.91 = (bf16[36,512]{1,0:T(8,128)(2,1)S(1)}, bf16[36,512]{1,0:T(8,128)(2,1)S(1)}, bf16[36,512]{1,0:T(8,128)(2,1)S(1)}, bf16[36,512]{1,0:T(8,128)(2,1)S(1)}) custom-call(bf16[1,12,12,512]{3,2,1,0:T(8,128)(2,1)} %tokens.1, f32[1,16,529]{2,1,0:T(8,128)} %table.2, f32[1,512]{1,0:T(1,128)} %bitcast.3, bf16[512,1536]{1,0:T(8,128)(2,1)} %wqkv.2, ...), custom_call_target="tpu_custom_call" | custom-call | flops 400000000 | bytes 2500000 | tf_op jit(solution)/shard_map/pallas_call | solution.py:329
  3.7 0.0 copy-start
  3.7 6.1 %collective-permute-start = (bf16[36,512]{1,0:T(8,128)(2,1)S(1)}, bf16[36,512]{1,0:T(8,128)(2,1)S(1)}, u32[]{:S(2)}, u32[]{:S(2)}) collective-permute-start(bf16[36,512]{1,0:T(8,128)(2,1)S(1)} %get-tuple-element.14), channel_id=1, source_target_pairs={{1,0},{2,1},{3,2},{4,3},{5,4},{6,5},{7,6},{0,7},{9,8},{10,9},{11,1... | collective-permute-start | bytes 110600 | tf_op jit(solution)/shard_map/ppermute | solution.py:365
  9.8 0.6 %collective-permute-start.1 = (bf16[36,512]{1,0:T(8,128)(2,1)S(1)}, bf16[36,512]{1,0:T(8,128)(2,1)S(1)}, u32[]{:S(2)}, u32[]{:S(2)}) collective-permute-start(bf16[36,512]{1,0:T(8,128)(2,1)S(1)} %get-tuple-element.15), channel_id=1, source_target_pairs={{8,0},{9,1},{10,2},{11,3},{12,4},{13,5},{14,6},{15,7},{16,8},{17,9... | collective-permute-start | bytes 110600 | tf_op jit(solution)/shard_map/ppermute | solution.py:365
  10.4 0.9 %collective-permute-start.2 = (bf16[36,512]{1,0:T(8,128)(2,1)S(1)}, bf16[36,512]{1,0:T(8,128)(2,1)S(1)}, u32[]{:S(2)}, u32[]{:S(2)}) collective-permute-start(bf16[36,512]{1,0:T(8,128)(2,1)S(1)} %get-tuple-element.16), channel_id=1, source_target_pairs={{9,0},{10,1},{11,2},{12,3},{13,4},{14,5},{15,6},{8,7},{17,8},{18,9... | collective-permute-start | bytes 110600 | tf_op jit(solution)/shard_map/ppermute | solution.py:365
  11.4 0.0 copy-done.2
  11.4 0.9 %shard_map.92.bias = f32[8,3,18,8,128]{4,3,2,1,0:T(8,128)S(1)} custom-call(f32[1,16,529]{2,1,0:T(8,128)S(1)} %copy-done.2), custom_call_target="tpu_custom_call" | custom-call | flops 2000000 | bytes 1800000 | tf_op jit(solution)/shard_map/pallas_call | solution.py:300
  12.3 0.0 collective-permute-done.ne_in
  12.3 0.0 collective-permute-done.1.sw_in
  12.3 1.6 %collective-permute-done.2.se_in = bf16[36,512]{1,0:T(8,128)(2,1)S(1)} collective-permute-done((bf16[36,512]{1,0:T(8,128)(2,1)S(1)}, bf16[36,512]{1,0:T(8,128)(2,1)S(1)}, u32[]{:S(2)}, u32[]{:S(2)}) %collective-permute-start.2) | collective-permute-done | bytes 36896 | tf_op jit(solution)/shard_map/ppermute | solution.py:365
  13.9 0.0 copy-done.1
  13.9 0.0 copy-done.3
  13.9 0.0 copy-done
  13.9 2.1 %shard_map.93 = (bf16[36,512]{1,0:T(8,128)(2,1)S(1)}, bf16[36,512]{1,0:T(8,128)(2,1)S(1)}, bf16[36,512]{1,0:T(8,128)(2,1)S(1)}, bf16[36,512]{1,0:T(8,128)(2,1)S(1)}) custom-call(bf16[36,512]{1,0:T(8,128)(2,1)S(1)} %get-tuple-element.13.nw_in, bf16[36,512]{1,0:T(8,128)(2,1)S(1)} %collective-permute-done.ne_in, ...), custom_call_target="tpu_custom_call" | custom-call | flops 400000000 | bytes 2500000 | tf_op jit(solution)/shard_map/pallas_call | solution.py:329
  16.0 0.1 collective-permute-start.3
  16.1 0.8 %collective-permute-start.4 = (bf16[36,512]{1,0:T(8,128)(2,1)S(1)}, bf16[36,512]{1,0:T(8,128)(2,1)S(1)}, u32[]{:S(2)}, u32[]{:S(2)}) collective-permute-start(bf16[36,512]{1,0:T(8,128)(2,1)S(1)} %get-tuple-element.18), channel_id=1, source_target_pairs={{24,0},{25,1},{26,2},{27,3},{28,4},{29,5},{30,6},{31,7},{0,8},{1,9... | collective-permute-start | bytes 110600 | tf_op jit(solution)/shard_map/ppermute | solution.py:365
  16.9 0.0 collective-permute-start.5
  16.9 6.6 %collective-permute-done.3.nw = bf16[36,512]{1,0:T(8,128)(2,1)S(1)} collective-permute-done((bf16[36,512]{1,0:T(8,128)(2,1)S(1)}, bf16[36,512]{1,0:T(8,128)(2,1)S(1)}, u32[]{:S(2)}, u32[]{:S(2)}) %collective-permute-start.3) | collective-permute-done | bytes 36896 | tf_op jit(solution)/shard_map/ppermute | solution.py:365
  23.5 0.0 collective-permute-done.4.ne
  23.5 0.5 %collective-permute-done.5.sw = bf16[36,512]{1,0:T(8,128)(2,1)S(1)} collective-permute-done((bf16[36,512]{1,0:T(8,128)(2,1)S(1)}, bf16[36,512]{1,0:T(8,128)(2,1)S(1)}, u32[]{:S(2)}, u32[]{:S(2)}) %collective-permute-start.5) | collective-permute-done | bytes 36896 | tf_op jit(solution)/shard_map/ppermute | solution.py:365
  24.0 0.8 %shard_map.94 = bf16[1,12,12,512]{3,2,1,0:T(8,128)(2,1)} custom-call(bf16[36,512]{1,0:T(8,128)(2,1)S(1)} %collective-permute-done.3.nw, bf16[36,512]{1,0:T(8,128)(2,1)S(1)} %collective-permute-done.4.ne, bf16[36,512]{1,0:T(8,128)(2,1)S(1)} %collective-permute-done.5.sw, bf16[36,512]{1,0:T(8,128)(2,1)S(1)} %get-tuple-element.20.se), custom_call_target="tpu_custom_call" | custom-call | tf_op jit(solution)/shard_map/pallas_call | solution.py:347
Async XLA Ops:
  0.0 11.4 %copy-start.2 = (f32[1,16,529]{2,1,0:T(8,128)S(1)}, f32[1,16,529]{2,1,0:T(8,128)}, u32[]{:S(2)}) copy-start(f32[1,16,529]{2,1,0:T(8,128)} %table.3) | copy-start | bytes 101572
  0.0 13.9 %copy-start.1 = (bf16[512,512]{1,0:T(8,128)(2,1)S(1)}, bf16[512,512]{1,0:T(8,128)(2,1)}, u32[]{:S(2)}) copy-start(bf16[512,512]{1,0:T(8,128)(2,1)} %wproj.3) | copy-start | bytes 1572868
  0.0 13.9 %copy-start.3 = (f32[512]{0:T(512)S(1)}, f32[512]{0:T(512)}, u32[]{:S(2)}) copy-start(f32[512]{0:T(512)} %param.14) | copy-start | bytes 6148
  3.7 10.2 %copy-start = (bf16[512,1536]{1,0:T(8,128)(2,1)S(1)}, bf16[512,1536]{1,0:T(8,128)(2,1)}, u32[]{:S(2)}) copy-start(bf16[512,1536]{1,0:T(8,128)(2,1)} %wqkv.3) | copy-start | bytes 4718596
  3.7 8.6 %collective-permute-start = (bf16[36,512]{1,0:T(8,128)(2,1)S(1)}, bf16[36,512]{1,0:T(8,128)(2,1)S(1)}, u32[]{:S(2)}, u32[]{:S(2)}) collective-permute-start(bf16[36,512]{1,0:T(8,128)(2,1)S(1)} %get-tuple-element.14), channel_id=1, source_target_pairs={{1,0},{2,1},{3,2},{4,3},{5,4},{6,5},{7,6},{0,7},{9,8},{10,9},{11,1... | collective-permute-start | bytes 110600 | tf_op jit(solution)/shard_map/ppermute | solution.py:365
  9.8 2.5 %collective-permute-start.1 = (bf16[36,512]{1,0:T(8,128)(2,1)S(1)}, bf16[36,512]{1,0:T(8,128)(2,1)S(1)}, u32[]{:S(2)}, u32[]{:S(2)}) collective-permute-start(bf16[36,512]{1,0:T(8,128)(2,1)S(1)} %get-tuple-element.15), channel_id=1, source_target_pairs={{8,0},{9,1},{10,2},{11,3},{12,4},{13,5},{14,6},{15,7},{16,8},{17,9... | collective-permute-start | bytes 110600 | tf_op jit(solution)/shard_map/ppermute | solution.py:365
  10.4 3.4 %collective-permute-start.2 = (bf16[36,512]{1,0:T(8,128)(2,1)S(1)}, bf16[36,512]{1,0:T(8,128)(2,1)S(1)}, u32[]{:S(2)}, u32[]{:S(2)}) collective-permute-start(bf16[36,512]{1,0:T(8,128)(2,1)S(1)} %get-tuple-element.16), channel_id=1, source_target_pairs={{9,0},{10,1},{11,2},{12,3},{13,4},{14,5},{15,6},{8,7},{17,8},{18,9... | collective-permute-start | bytes 110600 | tf_op jit(solution)/shard_map/ppermute | solution.py:365
  16.0 7.5 %collective-permute-start.3 = (bf16[36,512]{1,0:T(8,128)(2,1)S(1)}, bf16[36,512]{1,0:T(8,128)(2,1)S(1)}, u32[]{:S(2)}, u32[]{:S(2)}) collective-permute-start(bf16[36,512]{1,0:T(8,128)(2,1)S(1)} %get-tuple-element.17), channel_id=1, source_target_pairs={{31,0},{24,1},{25,2},{26,3},{27,4},{28,5},{29,6},{30,7},{7,8},{0,9... | collective-permute-start | bytes 110600 | tf_op jit(solution)/shard_map/ppermute | solution.py:365
  16.1 7.4 %collective-permute-start.4 = (bf16[36,512]{1,0:T(8,128)(2,1)S(1)}, bf16[36,512]{1,0:T(8,128)(2,1)S(1)}, u32[]{:S(2)}, u32[]{:S(2)}) collective-permute-start(bf16[36,512]{1,0:T(8,128)(2,1)S(1)} %get-tuple-element.18), channel_id=1, source_target_pairs={{24,0},{25,1},{26,2},{27,3},{28,4},{29,5},{30,6},{31,7},{0,8},{1,9... | collective-permute-start | bytes 110600 | tf_op jit(solution)/shard_map/ppermute | solution.py:365
  16.9 7.1 %collective-permute-start.5 = (bf16[36,512]{1,0:T(8,128)(2,1)S(1)}, bf16[36,512]{1,0:T(8,128)(2,1)S(1)}, u32[]{:S(2)}, u32[]{:S(2)}) collective-permute-start(bf16[36,512]{1,0:T(8,128)(2,1)S(1)} %get-tuple-element.19), channel_id=1, source_target_pairs={{7,0},{0,1},{1,2},{2,3},{3,4},{4,5},{5,6},{6,7},{15,8},{8,9},{9,10... | collective-permute-start | bytes 110600 | tf_op jit(solution)/shard_map/ppermute | solution.py:365
